TPU v7x, 256 devices: a whole 4x4x8 slice. The times are simulated.
256 devices in a mesh: ctx: 2 (over core), exp: 8 (over z), tp: 16 (over y, x).
Axes of the slice: x: 4, y: 4, z: 8, core: 2. Of those that a mesh axis runs over, the one named last changes fastest.
Arguments:
- conv_in: bfloat16 [8, 256, 4096], P('exp', 'ctx', 'tp'), may hold values from -6 to 6
- gate_in: bfloat16 [8, 256, 4096], P('exp', 'ctx', 'tp'), may hold values from -6 to 6
- residual: bfloat16 [8, 256, 2048], P('exp', 'ctx'), may hold values from -6 to 6
- conv_weight: float32 [4, 4096], P(None, 'tp'), may hold values from -3 to 3
- conv_bias: float32 [4096], P('tp'), may hold values from -3 to 3
- proj_weight: bfloat16 [4096, 288], P('tp'), may hold values from -0.09375 to 0.09375
- step_weight: bfloat16 [256, 4096], P(None, 'tp'), may hold values from -0.375 to 0.375
- step_bias: float32 [4096], P('tp'), may hold values from -6 to -2
- decay_log: float32 [16, 4096], P(None, 'tp'), may hold values from -3 to 2
- skip_gain: float32 [4096], P('tp'), may hold values from 0.5 to 1.5
- out_weight: bfloat16 [4096, 2048], P('tp'), may hold values from -0.09375 to 0.09375
- norm_gain: float32 [2048], replicated, may hold values from 0.5 to 1.5
- expert_ids: int32 [8, 256, 2], P('exp', 'ctx'), may hold values from 0 to 7, all different within a row; in each aligned block of 128 rows (0 to 127, 128 to 255, ..., all dimensions but the last counted through in order) at most 64 rows name the same one
- route_gates: float32 [8, 256, 2], P('exp', 'ctx'), may hold values from 0.2 to 1
- expert_weight: bfloat16 [8, 3, 2048, 14336], P('exp', None, None, ('ctx', 'tp')), may hold values from -0.125 to 0.125
Outputs:
- layer_out: bfloat16 [8, 256, 2048], P('exp', 'ctx', 'tp')
Inputs may be any that keep to these rules, and one draw needn't show every extreme that they name: `expert_ids`: the 2 picks of a token differ. Among the picks of the 128 tokens of one sequence block, no expert is named more than 64 times, and in some block one expert is named exactly 64 times.
All inputs are finite; a program needn't handle non-finite values.
Results may differ from a plain program's by a relative error of at most 0.015.
Values may be sent and summed in bfloat16 or wider, within the bound.
A program may use at most 128 MiB of HBM per device.

v0:
```python
import math

import jax
import jax.numpy as jnp
from jax import lax
from jax.sharding import PartitionSpec as P

D = 2048
STATE = 16
DT_RANK = 256
TOP = 2
CAP = 64


def from_behind(block, axis, distance):
    devices = range(lax.axis_size(axis))
    route = [(i - distance, i) for i in devices if i - distance in devices]
    return lax.ppermute(block, axis, route)


def prefix(value, axis, join, neutral):
    count, mine = (lax.axis_size(axis), lax.axis_index(axis))
    pieces = jax.tree.map(lambda part: lax.all_gather(part, axis), value)
    running = jax.tree.map(
        lambda part, zero: jnp.full_like(part, 0) + jnp.asarray(zero, part.dtype), value, neutral
    )

    def hop(position, running):
        longer = join(running, jax.tree.map(lambda part: part[position], pieces))
        return jax.tree.map(lambda new, old: jnp.where(position < mine, new, old), longer, running)

    return lax.fori_loop(0, count - 1, hop, running)


def chain_pair(earlier, later):
    return (earlier[0] * later[0], later[0] * earlier[1] + later[1])


def body(
    conv_in,
    gate_in,
    residual,
    conv_weight,
    conv_bias,
    proj_weight,
    step_weight,
    step_bias,
    decay_log,
    skip_gain,
    out_weight,
    norm_gain,
    expert_ids,
    route_gates,
    expert_weight,
):
    highest = lax.Precision.HIGHEST
    local_x = conv_in[0]
    token_rows = local_x.shape[0]
    channels = local_x.shape[1]
    tap_count = conv_weight.shape[0]
    before = from_behind(local_x[token_rows - tap_count + 1 :], "ctx", 1)
    extended = jnp.concatenate([before, local_x], axis=0).astype(jnp.float32)
    convolved = conv_bias[None, :] + sum(
        (conv_weight[k][None, :] * extended[k : k + token_rows] for k in range(tap_count))
    )
    xconv = jax.nn.silu(convolved).astype(jnp.bfloat16)
    projected = lax.psum(jnp.dot(xconv, proj_weight, preferred_element_type=jnp.float32), "tp")
    rank_part = projected[:, :DT_RANK].astype(jnp.bfloat16)
    input_map = projected[:, DT_RANK : DT_RANK + STATE]
    output_map = projected[:, DT_RANK + STATE :]
    step_sizes = jax.nn.softplus(
        jnp.dot(rank_part, step_weight, preferred_element_type=jnp.float32) + step_bias
    )
    decay_rates = -jnp.exp(decay_log)
    xfloat = xconv.astype(jnp.float32)
    driven = step_sizes * xfloat
    span = math.gcd(token_rows, 16)
    block_total = token_rows // span

    def run_block(state, pieces):
        steps_here, driven_here, in_here, out_here = pieces
        emitted = []
        for inner_step in range(span):
            state = (
                jnp.exp(steps_here[inner_step][None, :] * decay_rates) * state
                + driven_here[inner_step][None, :] * in_here[inner_step][:, None]
            )
            emitted.append(jnp.sum(out_here[inner_step][:, None] * state, axis=0))
        return (state, jnp.stack(emitted))

    pieces = (
        step_sizes.reshape(block_total, span, channels),
        driven.reshape(block_total, span, channels),
        input_map.reshape(block_total, span, STATE),
        output_map.reshape(block_total, span, STATE),
    )
    last_state, local_out = lax.scan(run_block, jnp.zeros((STATE, channels), jnp.float32), pieces)
    local_out = local_out.reshape(token_rows, channels)
    elapsed = jnp.cumsum(step_sizes, axis=0)
    last_decay = jnp.exp(elapsed[token_rows - 1][None, :] * decay_rates)
    incoming = prefix(
        (last_decay, last_state),
        "ctx",
        chain_pair,
        (jnp.ones_like(last_decay), jnp.zeros_like(last_state)),
    )[1]
    carried = jnp.sum(
        output_map[:, :, None] * jnp.exp(elapsed[:, None, :] * decay_rates[None]) * incoming[None],
        axis=1,
    )
    scanned = local_out + carried + skip_gain * xfloat
    gated = (scanned * jax.nn.silu(gate_in[0].astype(jnp.float32))).astype(jnp.bfloat16)
    partial_out = jnp.dot(gated, out_weight, preferred_element_type=jnp.float32)
    quarter = D // lax.axis_size("tp")
    lane_start = lax.axis_index("tp") * quarter
    expert_count = lax.axis_size("exp")
    picks = expert_ids[0]
    onehot = (picks[:, :, None] == jnp.arange(expert_count, dtype=jnp.int32)).astype(jnp.int32)
    flat_hot = onehot.reshape(token_rows * TOP, expert_count)
    ranks = jnp.cumsum(flat_hot, axis=0) - 1
    within = jnp.sum(ranks * flat_hot, axis=1).reshape(token_rows, TOP)
    places = picks * CAP + within
    table = (places[:, :, None] == jnp.arange(expert_count * CAP, dtype=jnp.int32)).astype(
        jnp.float32
    )
    chooser = jnp.sum(table, axis=1).astype(jnp.bfloat16)
    blender = jnp.sum(table * route_gates[0][:, :, None], axis=1)
    mixed = lax.psum_scatter(partial_out, "tp", scatter_dimension=1, tiled=True)
    own_residual = lax.dynamic_slice_in_dim(residual[0], lane_start, quarter, 1)
    stream = (own_residual.astype(jnp.float32) + mixed).astype(jnp.bfloat16)
    sfloat = stream.astype(jnp.float32)
    squares = lax.psum(jnp.sum(sfloat * sfloat, axis=1), "tp")
    own_gain = lax.dynamic_slice_in_dim(norm_gain, lane_start, quarter, 0)
    normed = (sfloat * lax.rsqrt(squares[:, None] / D + 1e-06) * own_gain).astype(jnp.bfloat16)
    picked = lax.dot_general(
        chooser, normed, (((0,), (0,)), ((), ())), preferred_element_type=jnp.float32
    )
    arrived = lax.all_to_all(
        picked.astype(jnp.bfloat16).reshape(expert_count, CAP, normed.shape[1]),
        "exp",
        split_axis=0,
        concat_axis=0,
        tiled=True,
    )
    arrived = lax.all_gather(arrived, "tp", axis=2, tiled=True)
    slot_rows = arrived.reshape(-1, D)
    local_weights = expert_weight[0]
    piece = lax.all_gather(local_weights, "ctx", axis=2, tiled=True)
    gate_part = jnp.dot(slot_rows, piece[0], preferred_element_type=jnp.float32)
    up_part = jnp.dot(slot_rows, piece[1], preferred_element_type=jnp.float32)
    hidden = (jax.nn.silu(gate_part) * up_part).astype(jnp.bfloat16)
    summed = jnp.zeros((slot_rows.shape[0], D), jnp.float32) + lax.dot_general(
        hidden, piece[2], (((1,), (1,)), ((), ())), preferred_element_type=jnp.float32
    )
    expert_out = (
        lax.psum_scatter(summed, "tp", scatter_dimension=1, tiled=True)
        .astype(jnp.bfloat16)
        .reshape(expert_count, CAP, quarter)
    )
    returned = lax.all_to_all(expert_out, "exp", split_axis=0, concat_axis=0, tiled=True)
    moe = jnp.dot(
        blender,
        returned.reshape(expert_count * CAP, quarter).astype(jnp.float32),
        precision=highest,
        preferred_element_type=jnp.float32,
    )
    final = (sfloat + moe).astype(jnp.bfloat16)
    return final[None]


def solution(mesh):
    placed = (
        P("exp", "ctx", "tp"),
        P("exp", "ctx", "tp"),
        P("exp", "ctx", None),
        P(None, "tp"),
        P("tp"),
        P("tp", None),
        P(None, "tp"),
        P("tp"),
        P(None, "tp"),
        P("tp"),
        P("tp", None),
        P(),
        P("exp", "ctx", None),
        P("exp", "ctx", None),
        P("exp", None, None, ("ctx", "tp")),
    )
    return jax.shard_map(
        body, mesh=mesh, in_specs=placed, out_specs=P("exp", "ctx", "tp"), check_vma=False
    )
```

profile of v0, /device:TPU:2, one launch (start us, length us, event | category | flops | bytes accessed | tf_op | source)
XLA Modules:
  0.0 459.3 jit_solution(14481502077356869707)
XLA Ops:
  6.5 0.8 slice_bitcast_fusion.10
  7.3 1.7 collective-permute-start
  9.1 0.8 fusion.63
  9.9 0.9 maximum_convert_fusion
  10.8 0.8 multiply_convert_fusion.1
  11.6 1.8 fusion.64
  13.4 96.1 %all-reduce.2.cloned.1.call-done = f32[128,288]{0,1:T(8,128)} async-done(((f32[128,288]{0,1:T(8,128)}), f32[128,288]{0,1:T(8,128)}) %all-reduce.2.cloned.1.call-update) | async-done | bytes 147472 | tf_op jit(solution)/shard_map/psum | solution.py:67
  109.5 0.7 fusion.62
  110.4 1.2 convert_multiply_fusion.2
  111.7 0.2 reduce_window_sum.24
  111.9 8.2 %while.3 = (s32[]{:T(128)}, f32[16,256]{1,0:T(8,128)S(1)}, f32[8,16,256]{2,1,0:T(8,128)S(1)}, f32[8,16,256]{2,1,0:T(8,128)S(1)}, f32[16,256]{1,0:T(8,128)S(1)}, ...) while((s32[]{:T(128)}, f32[16,256]{1,0:T(8,128)S(1)}, ...), condition=%wide.region_18.19_spmd.clone, body=%wide.region_1.18_spmd.clone.sunk | while | flops 577554 | bytes 505064 | solution.py:97
  111.9 0.2 fusion.77
  112.1 0.2 constant_dynamic-slice_fusion.65
  112.3 0.2 multiply_reduce_fusion.22
  112.6 0.1 multiply_reduce_fusion.25
  113.0 0.2 fusion.77
  113.1 0.2 constant_dynamic-slice_fusion.65
  113.3 0.2 multiply_reduce_fusion.22
  113.6 0.1 multiply_reduce_fusion.25
  114.0 0.2 fusion.77
  114.2 0.2 constant_dynamic-slice_fusion.65
  114.4 0.2 multiply_reduce_fusion.22
  115.0 0.2 fusion.77
  115.2 0.2 constant_dynamic-slice_fusion.65
  115.4 0.2 multiply_reduce_fusion.22
  116.1 0.2 fusion.77
  116.2 0.2 constant_dynamic-slice_fusion.65
  116.4 0.2 multiply_reduce_fusion.22
  117.1 0.2 fusion.77
  117.3 0.2 constant_dynamic-slice_fusion.65
  117.4 0.2 multiply_reduce_fusion.22
  118.1 0.2 fusion.77
  118.3 0.2 constant_dynamic-slice_fusion.65
  118.5 0.2 multiply_reduce_fusion.22
  119.1 0.2 fusion.77
  119.3 0.2 constant_dynamic-slice_fusion.65
  119.5 0.2 multiply_reduce_fusion.22
  120.2 1.8 all-gather
  122.0 1.8 all-gather.1
  123.8 0.7 multiply_reduce_fusion.16
  124.6 0.1 fusion.41
  124.7 1.3 fusion.65
  126.1 0.1 copy.31
  126.2 0.1 eq.43
  126.4 0.1 eq.39
  126.5 0.6 reduce-window.6
  127.1 0.2 slice_reduce_fusion
  127.5 0.1 reshape.246
  127.7 0.8 dynamic_slice.31
  128.5 0.2 convert_reduce_fusion
  128.6 76.4 %reduce-scatter.3.cloned.1.call-done = f32[128,128]{1,0:T(8,128)} async-done(((f32[128,2048]{1,0:T(8,128)}), f32[128,128]{1,0:T(8,128)}) %reduce-scatter.3.cloned.1.call-update) | async-done | bytes 65552 | tf_op jit(solution)/shard_map/reduce_scatter | solution.py:128
  205.1 0.9 fusion.50
  206.0 36.3 %psum.15 = f32[128]{0:T(128)S(1)} all-reduce(f32[128]{0:T(128)S(1)} %get-tuple-element.158), channel_id=1, replica_groups=mesh['ctx'=2,'exp'=8,'tp'=16] {'tp'}, use_global_device_ids=true, to_apply=%region_28.29 | all-reduce | flops 128 | bytes 1024 | tf_op jit(solution)/shard_map/psum | solution.py:132
  242.3 0.3 convolution_convert_fusion
  242.6 16.0 %all_to_all.10 = bf16[8,64,128]{2,1,0:T(8,128)(2,1)} all-to-all(bf16[8,64,128]{2,1,0:T(8,128)(2,1)S(1)} %bitcast.278), channel_id=1, replica_groups=mesh['ctx'=2,'exp'=8,'tp'=16] {'exp'}, dimensions={0} | all-to-all | bytes 262144 | tf_op jit(solution)/shard_map/all_to_all | solution.py:138
  258.7 0.5 all-gather.8.cloned.1.call-update
  259.2 44.6 %all-gather.6.cloned.1.call-done = bf16[8,64,2048]{2,1,0:T(8,128)(2,1)} async-done(((bf16[8,64,128]{2,1,0:T(8,128)(2,1)}), bf16[8,64,2048]{2,1,0:T(8,128)(2,1)}) %all-gather.6.cloned.1.call-update) | async-done | bytes 2097168 | tf_op jit(solution)/shard_map/all_gather | solution.py:145
  303.8 29.3 %all-gather.8.cloned.1.call-done = bf16[1,3,2048,896]{2,3,1,0:T(8,128)(2,1)} async-done(((bf16[1,3,2048,448]{2,3,1,0:T(8,128)(2,1)}), bf16[1,3,2048,896]{2,3,1,0:T(8,128)(2,1)}) %all-gather.8.cloned.1.call-update) | async-done | bytes 11010064 | tf_op jit(solution)/shard_map/all_gather | solution.py:148
  333.1 6.3 %fusion.35 = f32[512,896]{1,0:T(8,128)} fusion(bf16[512,2048]{1,0:T(8,128)(2,1)} %bitcast.364, bf16[1,3,2048,896]{2,3,1,0:T(8,128)(2,1)} %all-gather.8.cloned.1.call-done), kind=kOutput, calls=%fused_computation.135 | convolution fusion | flops 1879048192 | bytes 7602176 | tf_op jit(solution)/shard_map/dot_general | solution.py:149
  339.4 10.9 %fusion.33 = f32[512,2048]{1,0:T(8,128)} fusion(bf16[1,3,2048,896]{2,3,1,0:T(8,128)(2,1)} %all-gather.8.cloned.1.call-done, f32[512,896]{1,0:T(8,128)} %fusion.35, bf16[512,2048]{1,0:T(8,128)(2,1)} %bitcast.365), kind=kOutput, calls=%fused_computation.131 | convolution fusion | flops 3760848896 | bytes 15466496 | tf_op jit(solution)/shard_map/dot_general | solution.py:152
  350.4 84.7 %reduce-scatter.5.cloned.1.call-done = f32[512,128]{1,0:T(8,128)} async-done(((f32[512,2048]{1,0:T(8,128)}), f32[512,128]{1,0:T(8,128)}) %reduce-scatter.5.cloned.1.call-update) | async-done | bytes 262160 | tf_op jit(solution)/shard_map/reduce_scatter | solution.py:156
  435.1 1.0 convert_element_type.75
  436.0 15.9 %all_to_all.11 = bf16[8,64,128]{2,1,0:T(8,128)(2,1)S(1)} all-to-all(bf16[8,64,128]{2,1,0:T(8,128)(2,1)S(1)} %bitcast.277), channel_id=1, replica_groups=mesh['ctx'=2,'exp'=8,'tp'=16] {'exp'}, dimensions={0} | all-to-all | bytes 262144 | tf_op jit(solution)/shard_map/all_to_all | solution.py:160
  451.9 0.9 fusion.37
  (92 shorter events, 4.3 us)
Async XLA Ops:
  6.5 118.2 %copy-start = (bf16[256,2048]{1,0:T(8,128)(2,1)S(1)}, bf16[256,2048]{1,0:T(8,128)(2,1)}, u32[]{:S(2)}) copy-start(bf16[256,2048]{1,0:T(8,128)(2,1)} %param.27) | copy-start | bytes 3145732
  6.5 105.3 %copy-start.2 = (f32[16,256]{1,0:T(8,128)S(1)}, f32[16,256]{1,0:T(8,128)}, u32[]{:S(2)}) copy-start(f32[16,256]{1,0:T(8,128)} %param.25) | copy-start | bytes 49156
  6.5 103.0 %all-reduce.2.cloned.1.call-start = ((), (), s32[]{:S(2)}) async-start(), calls=%async_computation.4 | async-start | bytes 294912 | tf_op jit(solution)/shard_map/psum | solution.py:67
  7.3 2.6 collective-permute-start
  13.3 191.7 %reduce-scatter.3.cloned.1.call-start = ((), (), s32[]{:S(2)}) async-start(), calls=%async_computation.5 | async-start | bytes 1114112 | tf_op jit(solution)/shard_map/reduce_scatter | solution.py:128
  111.9 12.7 %copy-start.1 = (bf16[1,128,256]{2,1,0:T(8,128)(2,1)S(1)}, bf16[1,128,256]{2,1,0:T(8,128)(2,1)}, u32[]{:S(2)}) copy-start(bf16[1,128,256]{2,1,0:T(8,128)(2,1)} %param.18) | copy-start | bytes 196612
  111.9 12.6 %copy-start.3 = (f32[256]{0:T(256)S(1)}, f32[256]{0:T(256)}, u32[]{:S(2)}) copy-start(f32[256]{0:T(256)} %param.21) | copy-start | bytes 3076
  111.9 12.6 %copy-start.4 = (f32[256]{0:T(256)S(1)}, f32[256]{0:T(256)}, u32[]{:S(2)}) copy-start(f32[256]{0:T(256)} %param.26) | copy-start | bytes 3076
  124.5 1.6 copy-start.5
  124.7 3.8 copy-start.6
  126.1 177.8 %all-gather.6.cloned.1.call-start = ((), (), s32[]{:S(2)}) async-start(), calls=%async_computation.6 | async-start | bytes 2228224 | tf_op jit(solution)/shard_map/all_gather | solution.py:145
  258.6 74.5 %all-gather.8.cloned.1.call-start = ((), (), s32[]{:S(2)}) async-start(), calls=%async_computation.8 | async-start | bytes 16515072 | tf_op jit(solution)/shard_map/all_gather | solution.py:148
  259.2 175.9 %reduce-scatter.5.cloned.1.call-start = ((), (), s32[]{:S(2)}) async-start(), calls=%async_computation.7 | async-start | bytes 4456448 | tf_op jit(solution)/shard_map/reduce_scatter | solution.py:156
Sparse Core Ops, SparseCore 0:
  13.5 95.9 all-reduce.1
  126.2 78.8 reduce-scatter.2
  258.7 45.0 all-gather.5
  305.5 27.5 all-gather.7
  350.5 84.5 reduce-scatter.4
where the time goes:
time: 460 us; the launch traced here: 459 us
  waiting for transfers between devices  332 us (72%)
  blocking collectives  71.8 us (16%)
  matrix products  22.6 us (5%)
  between operations  13.4 us (3%)
  other arithmetic  10 us (2%)
  local copies, waits for them, and re-layouts  7.51 us (2%)
    psum x1, waiting for transfers between devices, body(): lax.psum(jnp.dot(xconv, proj_weight, preferred_element_type=jnp.float32),...  96.1 us
    reduce_scatter x1, waiting for transfers between devices, body(): lax.psum_scatter(summed, 'tp', scatter_dimension=1, tiled=True)  84.7 us
    reduce_scatter x1, waiting for transfers between devices, body(): mixed = lax.psum_scatter(partial_out, 'tp', scatter_dimension=1, tiled=True)  76.4 us
    all_gather x1, waiting for transfers between devices, body(): arrived = lax.all_gather(arrived, 'tp', axis=2, tiled=True)  44.6 us
    psum x1, blocking collectives, body(): squares = lax.psum(jnp.sum(sfloat * sfloat, axis=1), 'tp')  36.3 us
    all_gather x1, waiting for transfers between devices, body(): piece = lax.all_gather(local_weights, 'ctx', axis=2, tiled=True)  29.3 us
    all_to_all x1, blocking collectives, body(): lax.all_to_all(picked.astype(jnp.bfloat16).reshape(expert_count, CAP, nor...  16 us
    all_to_all x1, blocking collectives, body(): lax.all_to_all(expert_out, 'exp', split_axis=0, concat_axis=0, tiled=True)  15.9 us
  transfers between devices with their start and end apart: 6, of which 5 were waited for; matrix products, arithmetic and copies ran while one was open for 1% of the time, Pallas kernels for 0%

commit v1 on v0

v1 whole, which is shorter than its diff:
```python
import functools

import jax
import jax.numpy as jnp
from jax import lax
from jax.experimental import pallas as pl
from jax.experimental.pallas import tpu as pltpu
from jax.sharding import PartitionSpec as P

F32, BF16 = jnp.float32, jnp.bfloat16
D = 2048
STATE = 16
RANK = 256
CAP = 64
TOKENS = 128
CHANNELS = 256
HIDDEN = 448
SIDE = 4
TP = 16
EXP = 8
ROWS = EXP * CAP
GROUP = ROWS // 2
NEAR = (0, 1, 7, 2, 6, 3, 5, 4)
PEERS = [(dy, dx) for dy in (2, 1, 3, 0) for dx in (2, 1, 3, 0) if (dy, dx) != (0, 0)]


def dot(a, b, dims=((1,), (0,))):
    return lax.dot_general(a, b, (dims, ((), ())), preferred_element_type=F32)


def silu(v):
    return v * jax.nn.sigmoid(v)


def kernel(
    conv_in, gate_in, residual, conv_w, conv_b, proj_w, step_w, step_b, decay_log, skip, out_w, gain, ids, gates, experts,
    out,
    halo, ext, psend, precv, pall, mb, steps, driven, ys, hend, hstart, ow, res, osend, orecv, picked, xs, xn, wv, hid, rsend, rrecv, ret_send, ret,
    local_sem, ctx_send, ctx_recv, p_send, p_recv, a_send, a_recv, o_send, o_recv, z_send, z_recv, g_send, g_recv, r_send, r_recv, b_send, b_recv,
):
    core, z, tp = lax.axis_index("ctx"), lax.axis_index("exp"), lax.axis_index("tp")
    my_y, my_x = tp // SIDE, lax.rem(tp, SIDE)
    partner = {"ctx": 1 - core}

    def peer_of(dy, dx):
        return lax.rem(my_y + dy, SIDE) * SIDE + lax.rem(my_x + dx, SIDE)

    def remote(src, dst, ss, rs, device):
        return pltpu.make_async_remote_copy(
            src_ref=src, dst_ref=dst, send_sem=ss, recv_sem=rs, device_id=device, device_id_type=pl.DeviceIdType.MESH
        )

    my_lanes = pl.ds(pl.multiple_of(tp * 128, 128), 128)
    load_ow = pltpu.make_async_copy(out_w, ow, local_sem.at[0])
    load_res = pltpu.make_async_copy(residual.at[:, my_lanes], res, local_sem.at[1])
    load_wv = pltpu.make_async_copy(experts, wv.at[0], local_sem.at[2])
    load_ow.start()
    load_res.start()
    load_wv.start()

    barrier = pltpu.get_barrier_semaphore()
    pl.semaphore_signal(barrier, inc=1, device_id=partner, device_id_type=pl.DeviceIdType.MESH)
    for dy, dx in PEERS:
        pl.semaphore_signal(barrier, inc=1, device_id={"tp": peer_of(dy, dx)}, device_id_type=pl.DeviceIdType.MESH)
    for k in range(1, EXP):
        pl.semaphore_signal(barrier, inc=1, device_id={"exp": lax.rem(z + k, EXP)}, device_id_type=pl.DeviceIdType.MESH)
    pl.semaphore_wait(barrier, 1 + len(PEERS) + EXP - 1)

    send_halo = remote(conv_in.at[pl.ds(TOKENS - 16, 16)], halo, ctx_send.at[0], ctx_recv.at[0], partner)

    @pl.when(core == 0)
    def _():
        send_halo.start()
        halo[...] = jnp.zeros_like(halo)

    ext[pl.ds(8, TOKENS), :] = conv_in[...].astype(F32)

    @pl.when(core == 1)
    def _():
        send_halo.wait_recv()

    ext[pl.ds(0, 8), :] = halo[...].astype(F32)[8:16]
    convolved = conv_b[...] + sum(conv_w[pl.ds(k, 1), :] * ext[pl.ds(5 + k, TOKENS), :] for k in range(4))
    xconv = silu(convolved).astype(BF16)

    part = dot(xconv, proj_w[...], ((1,), (1,))).reshape(TP, 8, RANK + 2 * STATE)
    psend[...] = part.astype(BF16)
    copies = []
    for i, (dy, dx) in enumerate(PEERS):
        peer = peer_of(dy, dx)
        c = remote(psend.at[peer], precv.at[i], p_send.at[i], p_recv.at[i], {"tp": peer})
        c.start()
        copies.append(c)

    expert = lax.broadcasted_iota(jnp.int32, (EXP, TOKENS), 0)
    hot = [(expert == ids[pl.ds(p, 1), :]).astype(F32) for p in range(2)]
    row = lax.broadcasted_iota(jnp.int32, (TOKENS, TOKENS), 0)
    col = lax.broadcasted_iota(jnp.int32, (TOKENS, TOKENS), 1)
    counts = dot((hot[0] + hot[1]).astype(BF16), (row < col).astype(BF16))
    slot = lax.broadcasted_iota(jnp.int32, (ROWS, TOKENS), 0).astype(F32)
    taken = [
        (slot == ids[pl.ds(p, 1), :].astype(F32) * CAP + jnp.sum(hot[p] * counts, axis=0, keepdims=True)).astype(F32)
        for p in range(2)
    ]
    chooser = (taken[0] + taken[1]).astype(BF16)
    blend = taken[0] * gates[pl.ds(0, 1), :] + taken[1] * gates[pl.ds(1, 1), :]
    blend_hi = blend.astype(BF16)
    blend_lo = (blend - blend_hi.astype(F32)).astype(BF16)
    xfloat = xconv.astype(F32)
    gate = silu(gate_in[...].astype(F32))

    total = psend[tp].astype(F32)
    for i, c in enumerate(copies):
        c.wait_recv()
        total = total + precv[i].astype(F32)
    for c in copies:
        c.wait_send()
    pall[tp] = total.astype(BF16)
    copies = []
    for i, (dy, dx) in enumerate(PEERS):
        c = remote(pall.at[tp], pall.at[tp], a_send.at[i], a_recv.at[i], {"tp": peer_of(dy, dx)})
        c.start()
        copies.append(c)
    for c in copies:
        c.wait_send()
    for c in copies:
        c.wait_recv()
    projected = pall[...].astype(F32).reshape(TOKENS, RANK + 2 * STATE)
    rank_part = projected[:, :RANK].astype(BF16)
    maps = projected[:, RANK:]

    eye = (
        lax.broadcasted_iota(jnp.int32, (2 * STATE, 2 * STATE), 0) == lax.broadcasted_iota(jnp.int32, (2 * STATE, 2 * STATE), 1)
    ).astype(F32)
    spread = (maps[:, None, :] * eye[None]).reshape(TOKENS * 2 * STATE, 2 * STATE).astype(BF16)
    mb[...] = dot(spread, jnp.ones((2 * STATE, 128), BF16)).reshape(TOKENS, 2 * STATE, 128)

    raw = dot(rank_part, step_w[...]) + step_b[...]
    step_sizes = jnp.maximum(raw, 0.0) + jnp.log1p(jnp.exp(-jnp.abs(raw)))
    steps[...] = step_sizes
    driven[...] = step_sizes * xfloat
    decay = -jnp.exp(decay_log[...])
    send_state = remote(hend, hstart, ctx_send.at[1], ctx_recv.at[1], partner)

    @pl.when(core == 0)
    def _():
        hstart[...] = jnp.zeros_like(hstart)

    @pl.when(core == 1)
    def _():
        send_state.wait_recv()

    def scan_block(block, h):
        for i in range(8):
            t = block * 8 + i
            m = mb[t]
            in_map = jnp.concatenate([m[:STATE], m[:STATE]], axis=1)
            out_map = jnp.concatenate([m[STATE:], m[STATE:]], axis=1)
            h = jnp.exp(steps[pl.ds(t, 1), :] * decay) * h + driven[pl.ds(t, 1), :] * in_map
            ys[pl.ds(t, 1), :] = jnp.sum(out_map * h, axis=0, keepdims=True)
        return h

    hend[...] = lax.fori_loop(0, TOKENS // 8, scan_block, hstart[...])

    @pl.when(core == 0)
    def _():
        send_state.start()

    send_w = remote(experts, wv.at[1], ctx_send.at[2], ctx_recv.at[2], partner)
    send_w.start()
    gated = ((ys[...] + skip[...] * xfloat) * gate).astype(BF16)

    load_ow.wait()
    load_res.wait()
    copies = []
    i = 0
    for dy in (2, 1, 3, 0):
        yy = lax.rem(my_y + dy, SIDE)
        piece = dot(gated, ow[:, pl.ds(pl.multiple_of(yy * 512, 512), 512)])
        for j in range(SIDE):
            osend[yy * SIDE + j] = piece[:, j * 128 : (j + 1) * 128].astype(BF16)
        for dx in (2, 1, 3, 0):
            if (dy, dx) == (0, 0):
                continue
            peer = peer_of(dy, dx)
            c = remote(osend.at[peer], orecv.at[i], o_send.at[i], o_recv.at[i], {"tp": peer})
            c.start()
            copies.append(c)
            i += 1
    mixed = osend[tp].astype(F32)
    for i, c in enumerate(copies):
        c.wait_recv()
        mixed = mixed + orecv[i].astype(F32)
    stream = (res[...].astype(F32) + mixed).astype(BF16)

    chosen = dot(chooser, stream).astype(BF16).reshape(EXP, CAP, 128)
    picked[...] = chosen
    zcopies = [None] * EXP
    for pos, k in enumerate(NEAR):
        if k:
            dest = lax.rem(z + EXP - k, EXP)
            c = remote(picked.at[dest], xs.at[pl.ds(pos * CAP, CAP), my_lanes], z_send.at[pos], z_recv.at[pos], {"exp": dest})
            c.start()
            zcopies[pos] = c
    keep = pltpu.make_async_copy(picked.at[z], xs.at[pl.ds(0, CAP), my_lanes], local_sem.at[3])
    keep.start()
    keep.wait()
    gcopies = []
    for g in range(2):
        for pos in range(g * 4, g * 4 + 4):
            if zcopies[pos] is not None:
                zcopies[pos].wait_recv()
        block = xs.at[pl.ds(g * GROUP, GROUP), my_lanes]
        mine = []
        for i, (dy, dx) in enumerate(PEERS):
            c = remote(block, block, g_send.at[g, i], g_recv.at[g, i], {"tp": peer_of(dy, dx)})
            c.start()
            mine.append(c)
        gcopies.append(mine)
    for c in copies:
        c.wait_send()
    load_wv.wait()

    rcopies = []
    for g in range(2):
        for c in gcopies[g]:
            c.wait_recv()

        def norm_rows(r, _, g=g):
            at = pl.ds(pl.multiple_of(g * GROUP + r * 16, 16), 16)
            rows = xs[at, :].astype(F32)
            scale = lax.rsqrt(jnp.mean(rows * rows, axis=1, keepdims=True) + 1e-06)
            xn[pl.ds(pl.multiple_of(r * 16, 16), 16), :] = (rows * scale * gain[...]).astype(BF16)
            return 0

        lax.fori_loop(0, GROUP // 16, norm_rows, 0)
        if g == 0:
            send_w.wait_recv()

        def up_half(w, _):
            gate_part = dot(xn[...], wv[w, 0], ((1,), (1,)))
            up_part = dot(xn[...], wv[w, 1], ((1,), (1,)))
            hid[w] = (silu(gate_part) * up_part).astype(BF16)
            return 0

        lax.fori_loop(0, 2, up_half, 0)
        mine = []
        i = 0
        for dy in (2, 1, 3, 0):
            yy = lax.rem(my_y + dy, SIDE)
            down = pl.ds(pl.multiple_of(yy * 512, 512), 512)
            piece = dot(hid[0], wv[0, 2, :, down]) + dot(hid[1], wv[1, 2, :, down])
            for j in range(SIDE):
                rsend[g, yy * SIDE + j] = piece[:, j * 128 : (j + 1) * 128].astype(BF16)
            for dx in (2, 1, 3, 0):
                if (dy, dx) == (0, 0):
                    continue
                peer = peer_of(dy, dx)
                c = remote(rsend.at[g, peer], rrecv.at[g, i], r_send.at[g, i], r_recv.at[g, i], {"tp": peer})
                c.start()
                mine.append(c)
                i += 1
        rcopies.append(mine)

    bcopies = []
    for g in range(2):
        total = rsend[g, tp].astype(F32)
        for i, c in enumerate(rcopies[g]):
            c.wait_recv()
            total = total + rrecv[g, i].astype(F32)
        ret_send[pl.ds(g * GROUP, GROUP), :] = total.astype(BF16)
        for pos in range(g * 4, g * 4 + 4):
            k = NEAR[pos]
            src = ret_send.at[pl.ds(pos * CAP, CAP)]
            dst = ret.at[pl.ds(pl.multiple_of(z * CAP, CAP), CAP)]
            if k:
                c = remote(src, dst, b_send.at[pos], b_recv.at[pos], {"exp": lax.rem(z + k, EXP)})
            else:
                c = pltpu.make_async_copy(src, dst, local_sem.at[4])
            c.start()
            bcopies.append(c)
    for pos, c in enumerate(bcopies):
        if NEAR[pos]:
            c.wait_recv()
        else:
            c.wait()
    back = ret[...]
    moe = dot(blend_hi, back, ((0,), (0,))) + dot(blend_lo, back, ((0,), (0,)))
    out[...] = (stream.astype(F32) + moe).astype(BF16)

    @pl.when(core == 0)
    def _():
        send_halo.wait_send()
        send_state.wait_send()

    send_w.wait_send()
    for c in zcopies[1:] + gcopies[0] + gcopies[1] + rcopies[0] + rcopies[1]:
        c.wait_send()
    for pos, c in enumerate(bcopies):
        if NEAR[pos]:
            c.wait_send()


def body(
    conv_in, gate_in, residual, conv_weight, conv_bias, proj_weight, step_weight, step_bias, decay_log, skip_gain, out_weight, norm_gain,
    expert_ids, route_gates, expert_weight,
):
    vmem, hbm = pl.BlockSpec(memory_space=pltpu.VMEM), pl.BlockSpec(memory_space=pl.ANY)
    dma, n = pltpu.SemaphoreType.DMA, len(PEERS)
    wide = RANK + 2 * STATE
    result = pl.pallas_call(
        kernel,
        out_shape=jax.ShapeDtypeStruct((TOKENS, 128), BF16),
        in_specs=[vmem, vmem, hbm, vmem, vmem, vmem, vmem, vmem, vmem, vmem, hbm, vmem, vmem, vmem, hbm],
        out_specs=vmem,
        scratch_shapes=[
            pltpu.VMEM((16, CHANNELS), BF16),
            pltpu.VMEM((TOKENS + 8, CHANNELS), F32),
            pltpu.VMEM((TP, 8, wide), BF16),
            pltpu.VMEM((n, 8, wide), BF16),
            pltpu.VMEM((TP, 8, wide), BF16),
            pltpu.VMEM((TOKENS, 2 * STATE, 128), F32),
            pltpu.VMEM((TOKENS, CHANNELS), F32),
            pltpu.VMEM((TOKENS, CHANNELS), F32),
            pltpu.VMEM((TOKENS, CHANNELS), F32),
            pltpu.VMEM((STATE, CHANNELS), F32),
            pltpu.VMEM((STATE, CHANNELS), F32),
            pltpu.VMEM((CHANNELS, D), BF16),
            pltpu.VMEM((TOKENS, 128), BF16),
            pltpu.VMEM((TP, TOKENS, 128), BF16),
            pltpu.VMEM((n, TOKENS, 128), BF16),
            pltpu.VMEM((EXP, CAP, 128), BF16),
            pltpu.VMEM((ROWS, D), BF16),
            pltpu.VMEM((GROUP, D), BF16),
            pltpu.VMEM((2, 3, HIDDEN, D), BF16),
            pltpu.VMEM((2, GROUP, HIDDEN), BF16),
            pltpu.VMEM((2, TP, GROUP, 128), BF16),
            pltpu.VMEM((2, n, GROUP, 128), BF16),
            pltpu.VMEM((ROWS, 128), BF16),
            pltpu.VMEM((ROWS, 128), BF16),
            dma((5,)), dma((3,)), dma((3,)),
            dma((n,)), dma((n,)), dma((n,)), dma((n,)), dma((n,)), dma((n,)),
            dma((EXP,)), dma((EXP,)),
            dma((2, n)), dma((2, n)), dma((2, n)), dma((2, n)),
            dma((EXP,)), dma((EXP,)),
        ],
        compiler_params=pltpu.CompilerParams(collective_id=0, has_side_effects=True, vmem_limit_bytes=60 << 20),
        name="mixer_experts",
    )(
        conv_in[0], gate_in[0], residual[0], conv_weight, conv_bias[None], proj_weight.T, step_weight, step_bias[None], decay_log,
        skip_gain[None], out_weight, norm_gain[None], expert_ids[0].T, route_gates[0].T,
        jnp.swapaxes(expert_weight[0], 1, 2),
    )
    return result[None]


def solution(mesh):
    placed = (
        P("exp", "ctx", "tp"),
        P("exp", "ctx", "tp"),
        P("exp", "ctx", None),
        P(None, "tp"),
        P("tp"),
        P("tp", None),
        P(None, "tp"),
        P("tp"),
        P(None, "tp"),
        P("tp"),
        P("tp", None),
        P(),
        P("exp", "ctx", None),
        P("exp", "ctx", None),
        P("exp", None, None, ("ctx", "tp")),
    )
    return jax.shard_map(body, mesh=mesh, in_specs=placed, out_specs=P("exp", "ctx", "tp"), check_vma=False)
```

time: 460 us -> 98.8 us (0.21)
  the two profiles are of different devices: /device:TPU:2 before, /device:TPU:1 now
where the time goes in v1:
time: 98.8 us; the launch traced here: 98.6 us
  Pallas kernels  97.2 us (98%)
  local copies, waits for them, and re-layouts  1.38 us (1%)
    pallas_call x1, Pallas kernels, body(): pl.pallas_call(kernel, out_shape=jax.ShapeDtypeStruct((TOKENS, 128), BF16...  97.2 us

profile of v1, /device:TPU:1, one launch (start us, length us, event | category | flops | bytes accessed | tf_op | source)
XLA Modules:
  0.0 98.6 jit_solution(14954063957380377541)
XLA Ops:
  0.0 97.2 %mixer_experts.1 = bf16[128,128]{1,0:T(8,128)(2,1)} custom-call(bf16[128,256]{1,0:T(8,128)(2,1)} %bitcast.22, bf16[128,256]{1,0:T(8,128)(2,1)} %bitcast.23, bf16[128,2048]{1,0:T(8,128)(2,1)} %bitcast.19, f32[4,256]{1,0:T(4,128)} %conv_w.1, f32[1,256]{1,0:T(1,128)} %bitcast.25, bf16[288,256]{1,0:T(8,128)(2,1)} %bitcast.20, bf16[256,256]{1,0:T(8,128)(2,1)} %step_w.1, ...), custom_call_target="tpu_custom_call" | custom-call | tf_op jit(solution)/shard_map/mixer_experts/pallas_call | solution.py:311
  97.2 1.4 %copy.17 = bf16[1,128,128]{2,1,0:T(8,128)(2,1)} copy(bf16[1,128,128]{2,1,0:T(8,128)(2,1)} %bitcast.21) | data formatting | bytes 65536

commit v2 on v1

--- a/solution.py
+++ b/solution.py
@@ -35,8 +35,9 @@
 def kernel(
     conv_in, gate_in, residual, conv_w, conv_b, proj_w, step_w, step_b, decay_log, skip, out_w, gain, ids, gates, experts,
     out,
-    halo, ext, psend, precv, pall, mb, steps, driven, ys, hend, hstart, ow, res, osend, orecv, picked, xs, xn, wv, hid, rsend, rrecv, ret_send, ret,
-    local_sem, ctx_send, ctx_recv, p_send, p_recv, a_send, a_recv, o_send, o_recv, z_send, z_recv, g_send, g_recv, r_send, r_recv, b_send, b_recv,
+    halo, ext, psend, precv, pall, mb, steps, driven, ys, hend, hstart, ow, res, osend, orecv, picked, xs, xn, wv, hid, rsend, one, half_sum, two,
+    ret_send, ret,
+    local_sem, ctx_send, ctx_recv, p_send, p_recv, a_send, a_recv, o_send, o_recv, z_send, z_recv, g_send, g_recv, r_send, r_recv, q_send, q_recv, b_send, b_recv,
 ):
     core, z, tp = lax.axis_index("ctx"), lax.axis_index("exp"), lax.axis_index("tp")
     my_y, my_x = tp // SIDE, lax.rem(tp, SIDE)
@@ -205,80 +206,165 @@
     keep = pltpu.make_async_copy(picked.at[z], xs.at[pl.ds(0, CAP), my_lanes], local_sem.at[3])
     keep.start()
     keep.wait()
-    gcopies = []
-    for g in range(2):
-        for pos in range(g * 4, g * 4 + 4):
+    def chip(h, du, dv):
+        return peer_of((dv if h == 0 else du) % SIDE, (du if h == 0 else dv) % SIDE)
+
+    sent = []
+    FAR = (2, 1, 3)
+
+    def gather(g, h):
+        rows = pl.ds(g * GROUP + h * 128, 128)
+
+        def part_of(du, dv):
+            return xs.at[rows, pl.ds(pl.multiple_of(chip(h, du, dv) * 128, 128), 128)]
+
+        def put(m, to, origin):
+            ref = part_of(*origin)
+            c = remote(ref, ref, g_send.at[g, h, m], g_recv.at[g, h, m], {"tp": chip(h, *to)})
+            c.start()
+            sent.append(c)
+
+        def got(m, origin):
+            ref = part_of(*origin)
+            remote(ref, ref, g_send.at[g, h, m], g_recv.at[g, h, m], {"tp": tp}).wait_recv()
+
+        for pos in range(g * 4 + h * 2, g * 4 + h * 2 + 2):
             if zcopies[pos] is not None:
                 zcopies[pos].wait_recv()
-        block = xs.at[pl.ds(g * GROUP, GROUP), my_lanes]
-        mine = []
-        for i, (dy, dx) in enumerate(PEERS):
-            c = remote(block, block, g_send.at[g, i], g_recv.at[g, i], {"tp": peer_of(dy, dx)})
+        for d in FAR:
+            put(d - 1, (d, 0), (0, 0))
+        for d in FAR:
+            put(3 + d - 1, (0, d), (0, 0))
+        yield
+        for u in (1, 3, 2):
+            got(SIDE - u - 1, (u, 0))
+            for d in FAR:
+                put(3 + 3 * u + d - 1, (0, d), (u, 0))
+            yield
+        for u in range(SIDE):
+            for d in FAR:
+                got(3 + 3 * u + d - 1, (u, SIDE - d))
+        yield
+
+    def scatter(g, h):
+        my_a, my_b = (my_y, my_x) if h == 0 else (my_x, my_y)
+
+        def near(at, d):
+            return lax.rem(at + d, SIDE)
+
+        def tiles(d, q):
+            rows = pl.ds(h * 128 + q * 64, 64)
+            return rsend.at[g, near(my_a, d), :, rows, :] if h == 0 else rsend.at[g, :, near(my_a, d), rows, :]
+
+        def lane(d, q):
+            return half_sum.at[g, h, near(my_b, d), pl.ds(q * 64, 64), :]
+
+        def arrived(buf, ss, rs, q, d):
+            ref = buf.at[g, h, q, d - 1]
+            remote(ref, ref, ss.at[g, h, q, d - 1], rs.at[g, h, q, d - 1], {"tp": tp}).wait_recv()
+            return ref[...].astype(F32)
+
+        for d in FAR:
+            for q in range(2):
+                c = remote(tiles(d, q), one.at[g, h, q, d - 1], r_send.at[g, h, q, d - 1], r_recv.at[g, h, q, d - 1], {"tp": chip(h, 0, d)})
+                c.start()
+                sent.append(c)
+            yield
+        for q in range(2):
+            total = tiles(0, q)[...].astype(F32)
+            for d in range(1, SIDE):
+                total = total + arrived(one, r_send, r_recv, q, d)
+            half_sum[g, h, :, pl.ds(q * 64, 64), :] = total.astype(BF16)
+            for d in FAR:
+                c = remote(lane(d, q), two.at[g, h, q, d - 1], q_send.at[g, h, q, d - 1], q_recv.at[g, h, q, d - 1], {"tp": chip(h, d, 0)})
+                c.start()
+                sent.append(c)
+            yield
+        for q in range(2):
+            pos = g * 4 + h * 2 + q
+            total = lane(0, q)[...].astype(F32)
+            for d in range(1, SIDE):
+                total = total + arrived(two, q_send, q_recv, q, d)
+            rows = pl.ds(pos * CAP, CAP)
+            ret_send[rows, :] = total.astype(BF16)
+            dst = ret.at[pl.ds(pl.multiple_of(z * CAP, CAP), CAP)]
+            k = NEAR[pos]
+            if k:
+                c = remote(ret_send.at[rows], dst, b_send.at[pos], b_recv.at[pos], {"exp": lax.rem(z + k, EXP)})
+            else:
+                c = pltpu.make_async_copy(ret_send.at[rows], dst, local_sem.at[4])
             c.start()
-            mine.append(c)
-        gcopies.append(mine)
+            bcopies[pos] = c
+            yield
+
+    bcopies = [None] * EXP
+    gathers = [[gather(g, h) for h in range(2)] for g in range(2)]
+    scatters = [[scatter(g, h) for h in range(2)] for g in range(2)]
+
+    def step(pair):
+        for one_of in pair:
+            next(one_of)
+
+    step(gathers[0])
+    step(gathers[0])
+    step(gathers[0])
+    step(gathers[0])
+    step(gathers[1])
     for c in copies:
         c.wait_send()
     load_wv.wait()
-
-    rcopies = []
-    for g in range(2):
-        for c in gcopies[g]:
-            c.wait_recv()
-
-        def norm_rows(r, _, g=g):
-            at = pl.ds(pl.multiple_of(g * GROUP + r * 16, 16), 16)
-            rows = xs[at, :].astype(F32)
+    step(gathers[0])
+
+    def normalize(g):
+        def norm_rows(r, _):
+            rows = xs[pl.ds(pl.multiple_of(g * GROUP + r * 64, 64), 64), :].astype(F32)
             scale = lax.rsqrt(jnp.mean(rows * rows, axis=1, keepdims=True) + 1e-06)
-            xn[pl.ds(pl.multiple_of(r * 16, 16), 16), :] = (rows * scale * gain[...]).astype(BF16)
+            xn[pl.ds(pl.multiple_of(r * 64, 64), 64), :] = (rows * scale * gain[...]).astype(BF16)
             return 0
 
-        lax.fori_loop(0, GROUP // 16, norm_rows, 0)
-        if g == 0:
-            send_w.wait_recv()
-
-        def up_half(w, _):
-            gate_part = dot(xn[...], wv[w, 0], ((1,), (1,)))
-            up_part = dot(xn[...], wv[w, 1], ((1,), (1,)))
-            hid[w] = (silu(gate_part) * up_part).astype(BF16)
-            return 0
-
-        lax.fori_loop(0, 2, up_half, 0)
-        mine = []
-        i = 0
+        lax.fori_loop(0, GROUP // 64, norm_rows, 0)
+
+    def up(w):
+        gate_part = dot(xn[...], wv[w, 0], ((1,), (1,)))
+        up_part = dot(xn[...], wv[w, 1], ((1,), (1,)))
+        hid[w] = (silu(gate_part) * up_part).astype(BF16)
+
+    def down(g, dy):
+        yy = lax.rem(my_y + dy, SIDE)
+        cols = pl.ds(pl.multiple_of(yy * 512, 512), 512)
+        piece = dot(hid[0], wv[0, 2, :, cols]) + dot(hid[1], wv[1, 2, :, cols])
+        for j in range(SIDE):
+            rsend[g, yy, j] = piece[:, j * 128 : (j + 1) * 128].astype(BF16)
+
+    def all_down(g):
         for dy in (2, 1, 3, 0):
-            yy = lax.rem(my_y + dy, SIDE)
-            down = pl.ds(pl.multiple_of(yy * 512, 512), 512)
-            piece = dot(hid[0], wv[0, 2, :, down]) + dot(hid[1], wv[1, 2, :, down])
-            for j in range(SIDE):
-                rsend[g, yy * SIDE + j] = piece[:, j * 128 : (j + 1) * 128].astype(BF16)
-            for dx in (2, 1, 3, 0):
-                if (dy, dx) == (0, 0):
-                    continue
-                peer = peer_of(dy, dx)
-                c = remote(rsend.at[g, peer], rrecv.at[g, i], r_send.at[g, i], r_recv.at[g, i], {"tp": peer})
-                c.start()
-                mine.append(c)
-                i += 1
-        rcopies.append(mine)
-
-    bcopies = []
-    for g in range(2):
-        total = rsend[g, tp].astype(F32)
-        for i, c in enumerate(rcopies[g]):
-            c.wait_recv()
-            total = total + rrecv[g, i].astype(F32)
-        ret_send[pl.ds(g * GROUP, GROUP), :] = total.astype(BF16)
-        for pos in range(g * 4, g * 4 + 4):
-            k = NEAR[pos]
-            src = ret_send.at[pl.ds(pos * CAP, CAP)]
-            dst = ret.at[pl.ds(pl.multiple_of(z * CAP, CAP), CAP)]
-            if k:
-                c = remote(src, dst, b_send.at[pos], b_recv.at[pos], {"exp": lax.rem(z + k, EXP)})
-            else:
-                c = pltpu.make_async_copy(src, dst, local_sem.at[4])
-            c.start()
-            bcopies.append(c)
+            down(g, dy)
+            if dy:
+                next(scatters[g][0])
+        for _ in range(3):
+            next(scatters[g][1])
+
+    normalize(0)
+    step(gathers[1])
+    step(gathers[1])
+    send_w.wait_recv()
+    up(0)
+    step(gathers[1])
+    up(1)
+    all_down(0)
+    step(gathers[1])
+    normalize(1)
+    up(0)
+    up(1)
+    all_down(1)
+    step(scatters[0])
+    step(scatters[0])
+    step(scatters[1])
+    step(scatters[0])
+    step(scatters[0])
+    step(scatters[1])
+    step(scatters[1])
+    step(scatters[1])
     for pos, c in enumerate(bcopies):
         if NEAR[pos]:
             c.wait_recv()
@@ -294,7 +380,7 @@
         send_state.wait_send()
 
     send_w.wait_send()
-    for c in zcopies[1:] + gcopies[0] + gcopies[1] + rcopies[0] + rcopies[1]:
+    for c in zcopies[1:] + sent:
         c.wait_send()
     for pos, c in enumerate(bcopies):
         if NEAR[pos]:
@@ -334,14 +420,17 @@
             pltpu.VMEM((GROUP, D), BF16),
             pltpu.VMEM((2, 3, HIDDEN, D), BF16),
             pltpu.VMEM((2, GROUP, HIDDEN), BF16),
-            pltpu.VMEM((2, TP, GROUP, 128), BF16),
-            pltpu.VMEM((2, n, GROUP, 128), BF16),
+            pltpu.VMEM((2, SIDE, SIDE, GROUP, 128), BF16),
+            pltpu.VMEM((2, 2, 2, 3, SIDE, 64, 128), BF16),
+            pltpu.VMEM((2, 2, SIDE, 128, 128), BF16),
+            pltpu.VMEM((2, 2, 2, 3, 64, 128), BF16),
             pltpu.VMEM((ROWS, 128), BF16),
             pltpu.VMEM((ROWS, 128), BF16),
             dma((5,)), dma((3,)), dma((3,)),
             dma((n,)), dma((n,)), dma((n,)), dma((n,)), dma((n,)), dma((n,)),
             dma((EXP,)), dma((EXP,)),
-            dma((2, n)), dma((2, n)), dma((2, n)), dma((2, n)),
+            dma((2, 2, 15)), dma((2, 2, 15)),
+            dma((2, 2, 2, 3)), dma((2, 2, 2, 3)), dma((2, 2, 2, 3)), dma((2, 2, 2, 3)),
             dma((EXP,)), dma((EXP,)),
         ],
         compiler_params=pltpu.CompilerParams(collective_id=0, has_side_effects=True, vmem_limit_bytes=60 << 20),

time: 98.8 us -> 81.6 us (0.83)
  the two profiles are of different devices: /device:TPU:1 before, /device:TPU:2 now
where the time goes in v2:
time: 81.6 us; the launch traced here: 81 us
  Pallas kernels  79.7 us (98%)
  local copies, waits for them, and re-layouts  1.38 us (2%)
    pallas_call x1, Pallas kernels, body(): pl.pallas_call(kernel, out_shape=jax.ShapeDtypeStruct((TOKENS, 128), BF16...  79.7 us

profile of v2, /device:TPU:2, one launch (start us, length us, event | category | flops | bytes accessed | tf_op | source)
XLA Modules:
  0.0 81.0 jit_solution(511303284148971832)
XLA Ops:
  0.0 79.7 %mixer_experts.1 = bf16[128,128]{1,0:T(8,128)(2,1)} custom-call(bf16[128,256]{1,0:T(8,128)(2,1)} %bitcast.22, bf16[128,256]{1,0:T(8,128)(2,1)} %bitcast.23, bf16[128,2048]{1,0:T(8,128)(2,1)} %bitcast.19, f32[4,256]{1,0:T(4,128)} %conv_w.1, f32[1,256]{1,0:T(1,128)} %bitcast.25, bf16[288,256]{1,0:T(8,128)(2,1)} %bitcast.20, bf16[256,256]{1,0:T(8,128)(2,1)} %step_w.1, ...), custom_call_target="tpu_custom_call" | custom-call | tf_op jit(solution)/shard_map/mixer_experts/pallas_call | solution.py:397
  79.7 1.4 %copy.17 = bf16[1,128,128]{2,1,0:T(8,128)(2,1)} copy(bf16[1,128,128]{2,1,0:T(8,128)(2,1)} %bitcast.21) | data formatting | bytes 65536

commit v3 on v2

--- a/solution.py
+++ b/solution.py
@@ -20,7 +20,9 @@
 EXP = 8
 ROWS = EXP * CAP
 GROUP = ROWS // 2
-NEAR = (0, 1, 7, 2, 6, 3, 5, 4)
+NEAR = (0, 1, 7, 2, 4, 6, 3, 5)
+UNITS = ((0, 32, 0), (32, 32, 1), (64, 64, 0), (128, 64, 1), (192, 32, 0), (224, 32, 1), (256, 128, 0), (384, 128, 1))
+SPREAD = (2, 3, 4, 5)
 PEERS = [(dy, dx) for dy in (2, 1, 3, 0) for dx in (2, 1, 3, 0) if (dy, dx) != (0, 0)]
 
 
@@ -33,11 +35,12 @@
 
 
 def kernel(
-    conv_in, gate_in, residual, conv_w, conv_b, proj_w, step_w, step_b, decay_log, skip, out_w, gain, ids, gates, experts,
+    conv_hbm, gate_hbm, residual, conv_w_hbm, conv_b_hbm, proj_w_hbm, step_w_hbm, step_b_hbm, decay_hbm, skip_hbm, out_w, gain_hbm, ids_hbm, gates_hbm, experts,
     out,
-    halo, ext, psend, precv, pall, mb, steps, driven, ys, hend, hstart, ow, res, osend, orecv, picked, xs, xn, wv, hid, rsend, one, half_sum, two,
+    conv_in, gate_in, conv_w, conv_b, proj_w, step_w, step_b, decay_log, skip, gain, ids, gates, xc,
+    halo, ext, psend, precv, pall, mb, steps, driven, ys, hend, hstart, ow, res, osend, orecv, ohalf, orecv2, picked, xs, xn, wv, hid, rsend, one, half_sum, two,
     ret_send, ret,
-    local_sem, ctx_send, ctx_recv, p_send, p_recv, a_send, a_recv, o_send, o_recv, z_send, z_recv, g_send, g_recv, r_send, r_recv, q_send, q_recv, b_send, b_recv,
+    in_sem, local_sem, ctx_send, ctx_recv, p_send, p_recv, a_send, a_recv, o_send, o_recv, z_send, z_recv, g_send, g_recv, r_send, r_recv, q_send, q_recv, b_send, b_recv,
 ):
     core, z, tp = lax.axis_index("ctx"), lax.axis_index("exp"), lax.axis_index("tp")
     my_y, my_x = tp // SIDE, lax.rem(tp, SIDE)
@@ -46,46 +49,68 @@
     def peer_of(dy, dx):
         return lax.rem(my_y + dy, SIDE) * SIDE + lax.rem(my_x + dx, SIDE)
 
+    def chip(h, du, dv):
+        return peer_of((dv if h == 0 else du) % SIDE, (du if h == 0 else dv) % SIDE)
+
     def remote(src, dst, ss, rs, device):
         return pltpu.make_async_remote_copy(
             src_ref=src, dst_ref=dst, send_sem=ss, recv_sem=rs, device_id=device, device_id_type=pl.DeviceIdType.MESH
         )
 
     my_lanes = pl.ds(pl.multiple_of(tp * 128, 128), 128)
-    load_ow = pltpu.make_async_copy(out_w, ow, local_sem.at[0])
-    load_res = pltpu.make_async_copy(residual.at[:, my_lanes], res, local_sem.at[1])
-    load_wv = pltpu.make_async_copy(experts, wv.at[0], local_sem.at[2])
-    load_ow.start()
-    load_res.start()
-    load_wv.start()
-
     barrier = pltpu.get_barrier_semaphore()
-    pl.semaphore_signal(barrier, inc=1, device_id=partner, device_id_type=pl.DeviceIdType.MESH)
     for dy, dx in PEERS:
         pl.semaphore_signal(barrier, inc=1, device_id={"tp": peer_of(dy, dx)}, device_id_type=pl.DeviceIdType.MESH)
     for k in range(1, EXP):
         pl.semaphore_signal(barrier, inc=1, device_id={"exp": lax.rem(z + k, EXP)}, device_id_type=pl.DeviceIdType.MESH)
-    pl.semaphore_wait(barrier, 1 + len(PEERS) + EXP - 1)
-
-    send_halo = remote(conv_in.at[pl.ds(TOKENS - 16, 16)], halo, ctx_send.at[0], ctx_recv.at[0], partner)
+    for k, h in ((1, 0), (7, 1), (2, 0), (2, 1)):
+        for d in range(1, SIDE):
+            device = {"exp": lax.rem(z + k, EXP), "tp": chip(h, d, 0)}
+            pl.semaphore_signal(barrier, inc=1, device_id=device, device_id_type=pl.DeviceIdType.MESH)
+    pl.semaphore_signal(barrier, inc=1, device_id=partner, device_id_type=pl.DeviceIdType.MESH)
+    loads = [
+        pltpu.make_async_copy(src, dst, in_sem.at[i])
+        for i, (src, dst) in enumerate(
+            (
+                (conv_hbm, conv_in), (conv_w_hbm, conv_w), (conv_b_hbm, conv_b), (proj_w_hbm, proj_w), (ids_hbm, ids), (gates_hbm, gates),
+                (gate_hbm, gate_in), (step_w_hbm, step_w), (step_b_hbm, step_b), (decay_hbm, decay_log), (skip_hbm, skip), (gain_hbm, gain),
+            )
+        )
+    ]
+    load_ow = pltpu.make_async_copy(out_w, ow, local_sem.at[0])
+    load_res = pltpu.make_async_copy(residual.at[:, my_lanes], res, local_sem.at[1])
+    load_wv = pltpu.make_async_copy(experts, wv.at[0], local_sem.at[2])
+    for c in loads + [load_ow, load_res, load_wv]:
+        c.start()
+
+    def convolve(count):
+        convolved = conv_b[...] + sum(conv_w[pl.ds(k, 1), :] * ext[pl.ds(5 + k, count), :] for k in range(4))
+        return silu(convolved).astype(BF16)
+
+    def project(rows):
+        count = rows.shape[0]
+        return dot(rows, proj_w[...], ((1,), (1,))).reshape(count // 8, 8, RANK + 2 * STATE).astype(BF16)
+
+    for c in loads[:4]:
+        c.wait()
+    ext[pl.ds(0, 8), :] = jnp.zeros((8, CHANNELS), F32)
+    ext[pl.ds(8, TOKENS), :] = conv_in[...].astype(F32)
+    xc[...] = convolve(TOKENS)
+    psend[...] = project(xc[...])
+    pl.semaphore_wait(barrier, 1 + len(PEERS) + EXP - 1 + 12)
+    send_halo = remote(conv_hbm.at[pl.ds(TOKENS - 16, 16)], halo, ctx_send.at[0], ctx_recv.at[0], partner)
 
     @pl.when(core == 0)
     def _():
         send_halo.start()
-        halo[...] = jnp.zeros_like(halo)
-
-    ext[pl.ds(8, TOKENS), :] = conv_in[...].astype(F32)
 
     @pl.when(core == 1)
     def _():
         send_halo.wait_recv()
-
-    ext[pl.ds(0, 8), :] = halo[...].astype(F32)[8:16]
-    convolved = conv_b[...] + sum(conv_w[pl.ds(k, 1), :] * ext[pl.ds(5 + k, TOKENS), :] for k in range(4))
-    xconv = silu(convolved).astype(BF16)
-
-    part = dot(xconv, proj_w[...], ((1,), (1,))).reshape(TP, 8, RANK + 2 * STATE)
-    psend[...] = part.astype(BF16)
+        ext[pl.ds(0, 8), :] = halo[...].astype(F32)[8:16]
+        xc[pl.ds(0, 16), :] = convolve(16)
+        psend[pl.ds(0, 2)] = project(xc[pl.ds(0, 16), :])
+
     copies = []
     for i, (dy, dx) in enumerate(PEERS):
         peer = peer_of(dy, dx)
@@ -93,6 +118,8 @@
         c.start()
         copies.append(c)
 
+    for c in loads[4:]:
+        c.wait()
     expert = lax.broadcasted_iota(jnp.int32, (EXP, TOKENS), 0)
     hot = [(expert == ids[pl.ds(p, 1), :]).astype(F32) for p in range(2)]
     row = lax.broadcasted_iota(jnp.int32, (TOKENS, TOKENS), 0)
@@ -107,7 +134,7 @@
     blend = taken[0] * gates[pl.ds(0, 1), :] + taken[1] * gates[pl.ds(1, 1), :]
     blend_hi = blend.astype(BF16)
     blend_lo = (blend - blend_hi.astype(F32)).astype(BF16)
-    xfloat = xconv.astype(F32)
+    xfloat = xc[...].astype(F32)
     gate = silu(gate_in[...].astype(F32))
 
     total = psend[tp].astype(F32)
@@ -174,65 +201,99 @@
     load_ow.wait()
     load_res.wait()
     copies = []
-    i = 0
-    for dy in (2, 1, 3, 0):
+
+    def out_tiles(h, d):
+        at, rows = lax.rem((my_y if h == 0 else my_x) + d, SIDE), pl.ds(h * 64, 64)
+        return osend.at[at, :, rows, :] if h == 0 else osend.at[:, at, rows, :]
+
+    def out_send(src, dst, phase, h, d):
+        to = chip(h, 0, d) if phase == 0 else chip(h, d, 0)
+        c = remote(src, dst.at[h, d - 1], o_send.at[phase, h, d - 1], o_recv.at[phase, h, d - 1], {"tp": to})
+        c.start()
+        copies.append(c)
+
+    def out_arrived(buf, phase, h, d):
+        ref = buf.at[h, d - 1]
+        remote(ref, ref, o_send.at[phase, h, d - 1], o_recv.at[phase, h, d - 1], {"tp": tp}).wait_recv()
+        return ref[...].astype(F32)
+
+    for dy in (1, 3, 2, 0):
         yy = lax.rem(my_y + dy, SIDE)
         piece = dot(gated, ow[:, pl.ds(pl.multiple_of(yy * 512, 512), 512)])
         for j in range(SIDE):
-            osend[yy * SIDE + j] = piece[:, j * 128 : (j + 1) * 128].astype(BF16)
-        for dx in (2, 1, 3, 0):
-            if (dy, dx) == (0, 0):
-                continue
-            peer = peer_of(dy, dx)
-            c = remote(osend.at[peer], orecv.at[i], o_send.at[i], o_recv.at[i], {"tp": peer})
-            c.start()
-            copies.append(c)
-            i += 1
-    mixed = osend[tp].astype(F32)
-    for i, c in enumerate(copies):
-        c.wait_recv()
-        mixed = mixed + orecv[i].astype(F32)
+            osend[yy, j] = piece[:, j * 128 : (j + 1) * 128].astype(BF16)
+        if dy:
+            out_send(out_tiles(0, dy), orecv, 0, 0, dy)
+    for d in (1, 3, 2):
+        out_send(out_tiles(1, d), orecv, 0, 1, d)
+    for h in range(2):
+        total = out_tiles(h, 0)[...].astype(F32)
+        for d in range(1, SIDE):
+            total = total + out_arrived(orecv, 0, h, d)
+        ohalf[h] = total.astype(BF16)
+        for d in (1, 3, 2):
+            out_send(ohalf.at[h, lax.rem((my_x if h == 0 else my_y) + d, SIDE)], orecv2, 1, h, d)
+    mixed = []
+    for h in range(2):
+        total = ohalf[h, my_x if h == 0 else my_y].astype(F32)
+        for d in range(1, SIDE):
+            total = total + out_arrived(orecv2, 1, h, d)
+        mixed.append(total)
+    mixed = jnp.concatenate(mixed, axis=0)
     stream = (res[...].astype(F32) + mixed).astype(BF16)
 
     chosen = dot(chooser, stream).astype(BF16).reshape(EXP, CAP, 128)
     picked[...] = chosen
     zcopies = [None] * EXP
-    for pos, k in enumerate(NEAR):
-        if k:
-            dest = lax.rem(z + EXP - k, EXP)
-            c = remote(picked.at[dest], xs.at[pl.ds(pos * CAP, CAP), my_lanes], z_send.at[pos], z_recv.at[pos], {"exp": dest})
+    spread = []
+    for unit in SPREAD:
+        start, count, h = UNITS[unit]
+        pos = start // CAP
+        dest = lax.rem(z + EXP - NEAR[pos], EXP)
+        for d in (1, 3, 2, 0):
+            m = (d + 15) % 16 if d == 0 else d - 1
+            c = remote(
+                picked.at[dest, pl.ds(start - pos * CAP, count)],
+                xs.at[pl.ds(start, count), my_lanes],
+                g_send.at[unit, m],
+                g_recv.at[unit, m],
+                {"exp": dest, "tp": chip(h, d, 0)},
+            )
             c.start()
-            zcopies[pos] = c
+            spread.append(c)
+    for pos in range(4, EXP):
+        dest = lax.rem(z + EXP - NEAR[pos], EXP)
+        c = remote(picked.at[dest], xs.at[pl.ds(pos * CAP, CAP), my_lanes], z_send.at[pos], z_recv.at[pos], {"exp": dest})
+        c.start()
+        zcopies[pos] = c
     keep = pltpu.make_async_copy(picked.at[z], xs.at[pl.ds(0, CAP), my_lanes], local_sem.at[3])
     keep.start()
     keep.wait()
-    def chip(h, du, dv):
-        return peer_of((dv if h == 0 else du) % SIDE, (du if h == 0 else dv) % SIDE)
-
     sent = []
-    FAR = (2, 1, 3)
-
-    def gather(g, h):
-        rows = pl.ds(g * GROUP + h * 128, 128)
+    FAR = (1, 3, 2)
+
+    def gather(unit):
+        start, count, h = UNITS[unit]
+        rows = pl.ds(start, count)
 
         def part_of(du, dv):
             return xs.at[rows, pl.ds(pl.multiple_of(chip(h, du, dv) * 128, 128), 128)]
 
         def put(m, to, origin):
             ref = part_of(*origin)
-            c = remote(ref, ref, g_send.at[g, h, m], g_recv.at[g, h, m], {"tp": chip(h, *to)})
+            c = remote(ref, ref, g_send.at[unit, m], g_recv.at[unit, m], {"tp": chip(h, *to)})
             c.start()
             sent.append(c)
 
         def got(m, origin):
             ref = part_of(*origin)
-            remote(ref, ref, g_send.at[g, h, m], g_recv.at[g, h, m], {"tp": tp}).wait_recv()
-
-        for pos in range(g * 4 + h * 2, g * 4 + h * 2 + 2):
-            if zcopies[pos] is not None:
-                zcopies[pos].wait_recv()
-        for d in FAR:
-            put(d - 1, (d, 0), (0, 0))
+            remote(ref, ref, g_send.at[unit, m], g_recv.at[unit, m], {"tp": tp}).wait_recv()
+
+        if unit in SPREAD:
+            got(15, (0, 0))
+        else:
+            for d in (1, 3, 2):
+                put(d - 1, (d, 0), (0, 0))
         for d in FAR:
             put(3 + d - 1, (0, d), (0, 0))
         yield
@@ -240,7 +301,8 @@
             got(SIDE - u - 1, (u, 0))
             for d in FAR:
                 put(3 + 3 * u + d - 1, (0, d), (u, 0))
-            yield
+            if u != 1:
+                yield
         for u in range(SIDE):
             for d in FAR:
                 got(3 + 3 * u + d - 1, (u, SIDE - d))
@@ -264,11 +326,10 @@
             remote(ref, ref, ss.at[g, h, q, d - 1], rs.at[g, h, q, d - 1], {"tp": tp}).wait_recv()
             return ref[...].astype(F32)
 
-        for d in FAR:
-            for q in range(2):
-                c = remote(tiles(d, q), one.at[g, h, q, d - 1], r_send.at[g, h, q, d - 1], r_recv.at[g, h, q, d - 1], {"tp": chip(h, 0, d)})
-                c.start()
-                sent.append(c)
+        for q, d in [(q, d) for q in range(2) for d in FAR]:
+            c = remote(tiles(d, q), one.at[g, h, q, d - 1], r_send.at[g, h, q, d - 1], r_recv.at[g, h, q, d - 1], {"tp": chip(h, 0, d)})
+            c.start()
+            sent.append(c)
             yield
         for q in range(2):
             total = tiles(0, q)[...].astype(F32)
@@ -298,22 +359,34 @@
             yield
 
     bcopies = [None] * EXP
-    gathers = [[gather(g, h) for h in range(2)] for g in range(2)]
+    gathers = [[gather(2 * i), gather(2 * i + 1)] for i in range(4)]
     scatters = [[scatter(g, h) for h in range(2)] for g in range(2)]
 
     def step(pair):
         for one_of in pair:
             next(one_of)
 
-    step(gathers[0])
+    def landed(*positions):
+        for pos in positions:
+            zcopies[pos].wait_recv()
+
     step(gathers[0])
     step(gathers[0])
     step(gathers[0])
     step(gathers[1])
+    step(gathers[1])
+    step(gathers[1])
+    step(gathers[2])
+    step(gathers[2])
+    step(gathers[2])
+    landed(4, 5, 6, 7)
+    step(gathers[3])
+    step(gathers[0])
+    step(gathers[1])
+    step(gathers[2])
     for c in copies:
         c.wait_send()
     load_wv.wait()
-    step(gathers[0])
 
     def normalize(g):
         def norm_rows(r, _):
@@ -337,32 +410,32 @@
             rsend[g, yy, j] = piece[:, j * 128 : (j + 1) * 128].astype(BF16)
 
     def all_down(g):
-        for dy in (2, 1, 3, 0):
+        for dy in (1, 3, 2, 0):
             down(g, dy)
             if dy:
                 next(scatters[g][0])
-        for _ in range(3):
-            next(scatters[g][1])
+        for h in (1, 0, 1):
+            for _ in range(3):
+                next(scatters[g][h])
 
     normalize(0)
-    step(gathers[1])
-    step(gathers[1])
+    step(gathers[3])
     send_w.wait_recv()
     up(0)
-    step(gathers[1])
+    step(gathers[3])
     up(1)
     all_down(0)
-    step(gathers[1])
+    step(gathers[3])
     normalize(1)
     up(0)
     up(1)
+    step(scatters[0])
     all_down(1)
     step(scatters[0])
-    step(scatters[0])
+    step(scatters[1])
     step(scatters[1])
     step(scatters[0])
     step(scatters[0])
-    step(scatters[1])
     step(scatters[1])
     step(scatters[1])
     for pos, c in enumerate(bcopies):
@@ -380,7 +453,7 @@
         send_state.wait_send()
 
     send_w.wait_send()
-    for c in zcopies[1:] + sent:
+    for c in zcopies[4:] + spread + sent:
         c.wait_send()
     for pos, c in enumerate(bcopies):
         if NEAR[pos]:
@@ -397,9 +470,22 @@
     result = pl.pallas_call(
         kernel,
         out_shape=jax.ShapeDtypeStruct((TOKENS, 128), BF16),
-        in_specs=[vmem, vmem, hbm, vmem, vmem, vmem, vmem, vmem, vmem, vmem, hbm, vmem, vmem, vmem, hbm],
+        in_specs=[hbm] * 15,
         out_specs=vmem,
         scratch_shapes=[
+            pltpu.VMEM((TOKENS, CHANNELS), BF16),
+            pltpu.VMEM((TOKENS, CHANNELS), BF16),
+            pltpu.VMEM((4, CHANNELS), F32),
+            pltpu.VMEM((1, CHANNELS), F32),
+            pltpu.VMEM((wide, CHANNELS), BF16),
+            pltpu.VMEM((RANK, CHANNELS), BF16),
+            pltpu.VMEM((1, CHANNELS), F32),
+            pltpu.VMEM((STATE, CHANNELS), F32),
+            pltpu.VMEM((1, CHANNELS), F32),
+            pltpu.VMEM((1, D), F32),
+            pltpu.VMEM((2, TOKENS), jnp.int32),
+            pltpu.VMEM((2, TOKENS), F32),
+            pltpu.VMEM((TOKENS, CHANNELS), BF16),
             pltpu.VMEM((16, CHANNELS), BF16),
             pltpu.VMEM((TOKENS + 8, CHANNELS), F32),
             pltpu.VMEM((TP, 8, wide), BF16),
@@ -413,8 +499,10 @@
             pltpu.VMEM((STATE, CHANNELS), F32),
             pltpu.VMEM((CHANNELS, D), BF16),
             pltpu.VMEM((TOKENS, 128), BF16),
-            pltpu.VMEM((TP, TOKENS, 128), BF16),
-            pltpu.VMEM((n, TOKENS, 128), BF16),
+            pltpu.VMEM((SIDE, SIDE, TOKENS, 128), BF16),
+            pltpu.VMEM((2, 3, SIDE, 64, 128), BF16),
+            pltpu.VMEM((2, SIDE, 64, 128), BF16),
+            pltpu.VMEM((2, 3, 64, 128), BF16),
             pltpu.VMEM((EXP, CAP, 128), BF16),
             pltpu.VMEM((ROWS, D), BF16),
             pltpu.VMEM((GROUP, D), BF16),
@@ -426,10 +514,10 @@
             pltpu.VMEM((2, 2, 2, 3, 64, 128), BF16),
             pltpu.VMEM((ROWS, 128), BF16),
             pltpu.VMEM((ROWS, 128), BF16),
-            dma((5,)), dma((3,)), dma((3,)),
-            dma((n,)), dma((n,)), dma((n,)), dma((n,)), dma((n,)), dma((n,)),
+            dma((12,)), dma((5,)), dma((3,)), dma((3,)),
+            dma((n,)), dma((n,)), dma((n,)), dma((n,)), dma((2, 2, 3)), dma((2, 2, 3)),
             dma((EXP,)), dma((EXP,)),
-            dma((2, 2, 15)), dma((2, 2, 15)),
+            dma((len(UNITS), 16)), dma((len(UNITS), 16)),
             dma((2, 2, 2, 3)), dma((2, 2, 2, 3)), dma((2, 2, 2, 3)), dma((2, 2, 2, 3)),
             dma((EXP,)), dma((EXP,)),
         ],

time: 81.6 us -> 78.4 us (0.961)
  Pallas kernels: 79.7 us -> 76.5 us
    pallas_call x1, Pallas kernels: 79.7 us -> 76.5 us  [body(): pl.pallas_call(kernel, out_shape=jax.ShapeDtypeStruct((TOKENS, 128), BF16...]
where the time goes in v3:
time: 78.4 us; the launch traced here: 77.9 us
  Pallas kernels  76.5 us (98%)
  local copies, waits for them, and re-layouts  1.38 us (2%)
    pallas_call x1, Pallas kernels, body(): pl.pallas_call(kernel, out_shape=jax.ShapeDtypeStruct((TOKENS, 128), BF16...  76.5 us

profile of v3, /device:TPU:2, one launch (start us, length us, event | category | flops | bytes accessed | tf_op | source)
XLA Modules:
  0.0 77.9 jit_solution(17815561531764429461)
XLA Ops:
  0.0 76.5 %mixer_experts.1 = bf16[128,128]{1,0:T(8,128)(2,1)} custom-call(bf16[128,256]{1,0:T(8,128)(2,1)} %bitcast.22, bf16[128,256]{1,0:T(8,128)(2,1)} %bitcast.23, bf16[128,2048]{1,0:T(8,128)(2,1)} %bitcast.19, f32[4,256]{1,0:T(4,128)} %conv_w_hbm.1, f32[1,256]{1,0:T(1,128)} %bitcast.25, bf16[288,256]{1,0:T(8,128)(2,1)} %bitcast.20, bf16[256,256]{1,0:T(8,128)(2,1)} %step_w_hbm.1, ...), custom_call_target="tpu_custom_call" | custom-call | tf_op jit(solution)/shard_map/mixer_experts/pallas_call | solution.py:470
  76.5 1.4 %copy.17 = bf16[1,128,128]{2,1,0:T(8,128)(2,1)} copy(bf16[1,128,128]{2,1,0:T(8,128)(2,1)} %bitcast.21) | data formatting | bytes 65536
